TPU v7x, 32 devices: a whole 2x2x4 slice. The times are simulated.
32 devices in a mesh: dp: 4 (over z), mp: 8 (over y, x, core).
Axes of the slice: x: 2, y: 2, z: 4, core: 2. Of those that a mesh axis runs over, the one named last changes fastest.
Arguments:
- features: bfloat16 [192, 1664], P('dp'), may hold values from -6 to 6
- output_grad: bfloat16 [192, 1664], P('dp'), may hold values from -6 to 6
- send_rows: int32 [16, 12], P('dp'), may hold values from 0 to 48, as said below
- patches: int32 [16], replicated, may hold values from 0 to 12, as said below
- up_weight: float32 [6144, 1664], P(('dp', 'mp'))
- down_weight: float32 [6144, 1664], P(('dp', 'mp'))
- up_moment: float32 [6144, 1664], P(('dp', 'mp')), may hold values from -0.0006 to 0.0006
- down_moment: float32 [6144, 1664], P(('dp', 'mp')), may hold values from -0.0006 to 0.0006
- up_second: float32 [6144, 1664], P(('dp', 'mp')), may hold values from 1e-09 to 1e-07
- down_second: float32 [6144, 1664], P(('dp', 'mp')), may hold values from 1e-09 to 1e-07
Outputs:
- new_up: float32 [6144, 1664], P(('dp', 'mp'))
- new_down: float32 [6144, 1664], P(('dp', 'mp'))
- ratios: float32 [2], replicated
Inputs may be any that keep to these rules, and one draw needn't show every extreme that they name: `send_rows`: row d * 4 + p lists the rows of group d's block sent to group p, one a slot, 48 marking an empty slot. Group d's live rows are the first ones of its block, as many as the sum of its 4 patch counts; each live row is listed exactly once in group d's rows and no other row is listed. In every draw some group fills all its slots. `patches`: entries d * 4 to d * 4 + 3 are the patch counts of group d's images, 0 for an empty place; in every draw some group's counts sum to 48.
All inputs are finite; a program needn't handle non-finite values.
Results may differ from a plain program's by a relative error of at most 0.0003.
Values may be sent and summed in bfloat16 or wider, within the bound.
No kernel may reach another device: no remote copies, remote signals or barrier semaphores. Data moves between devices by JAX's collectives and lax.ppermute only.
A program may use at most 64 MiB of HBM per device.

v0:
```python
import math
import jax
import jax.numpy as jnp
from jax import lax
from jax.sharding import PartitionSpec as P

FF = 6144
IMGS = 4
inv_root_two = 1.0 / math.sqrt(2.0)
inv_root_tau = 1.0 / math.sqrt(2.0 * math.pi)
beta_first = 0.9
beta_second = 0.999
corr_first = 0.99997343860111
corr_second = 0.09520785288629
adam_eps = 1e-06
norm_eps = 1e-06
decay_rate = 0.05
learn_rate = 0.02


def gelu_exact(value):
    return 0.5 * value * (1.0 + lax.erf(value * inv_root_two))


def gelu_slope(value):
    return (
        0.5 * (1.0 + lax.erf(value * inv_root_two))
        + value * jnp.exp(-0.5 * value * value) * inv_root_tau
    )


def lamb_update(weight, grad, moment, second):
    moment_new = beta_first * moment + (1.0 - beta_first) * grad
    second_new = beta_second * second + (1.0 - beta_second) * grad * grad
    return (
        moment_new / corr_first / (jnp.sqrt(second_new / corr_second) + adam_eps)
        + decay_rate * weight
    )


def per_device(
    features,
    output_grad,
    send_rows,
    patches,
    up_weight,
    down_weight,
    up_moment,
    down_moment,
    up_second,
    down_second,
):
    width = features.shape[1]
    total = jnp.sum(patches).astype(jnp.float32)
    up_scale = 1.0 / math.sqrt(width)
    down_scale = 1.0 / math.sqrt(FF)
    group = lax.axis_index("dp")
    counts = lax.dynamic_slice_in_dim(patches, group * IMGS, IMGS)
    live = jnp.sum(counts)
    inside = (jnp.arange(features.shape[0], dtype=jnp.int32) < live)[:, None]
    inputs = jnp.where(inside, features, jnp.zeros_like(features))
    cotangent = jnp.where(inside, output_grad, jnp.zeros_like(output_grad))
    stacked = jnp.stack([up_weight.astype(jnp.bfloat16), down_weight.astype(jnp.bfloat16)])
    piece = lax.all_gather(stacked, "dp", axis=1, tiled=True)
    pre_part = (
        lax.dot_general(
            inputs, piece[0], (((1,), (1,)), ((), ())), preferred_element_type=jnp.float32
        )
        * up_scale
    )
    back_part = (
        lax.dot_general(
            cotangent, piece[1], (((1,), (1,)), ((), ())), preferred_element_type=jnp.float32
        )
        * down_scale
    )
    both = jnp.stack([pre_part, back_part])
    pre = both[0]
    hidden = gelu_exact(pre).astype(jnp.bfloat16)
    slope = (both[1] * gelu_slope(pre)).astype(jnp.bfloat16)
    up_term = lax.dot_general(
        slope, inputs, (((0,), (0,)), ((), ())), preferred_element_type=jnp.float32
    ) * (up_scale / total)
    down_term = lax.dot_general(
        hidden, cotangent, (((0,), (0,)), ((), ())), preferred_element_type=jnp.float32
    ) * (down_scale / total)
    summed = lax.psum_scatter(
        jnp.concatenate([up_term, down_term], 1).astype(jnp.bfloat16),
        "dp",
        scatter_dimension=0,
        tiled=True,
    ).astype(jnp.float32)
    update_up = lamb_update(up_weight, summed[:, :width], up_moment, up_second)
    update_down = lamb_update(down_weight, summed[:, width:], down_moment, down_second)
    weight_up_sq, update_up_sq, weight_down_sq, update_down_sq = lax.psum(
        (
            jnp.sum(up_weight * up_weight),
            jnp.sum(update_up * update_up),
            jnp.sum(down_weight * down_weight),
            jnp.sum(update_down * update_down),
        ),
        ("dp", "mp"),
    )
    ratio_up = jnp.sqrt(weight_up_sq / (update_up_sq + norm_eps))
    ratio_down = jnp.sqrt(weight_down_sq / (update_down_sq + norm_eps))
    new_up = up_weight - learn_rate * ratio_up * update_up
    new_down = down_weight - learn_rate * ratio_down * update_down
    return (new_up, new_down, jnp.stack([ratio_up, ratio_down]))


def solution(mesh):
    placed = (
        P("dp", None),
        P("dp", None),
        P("dp", None),
        P(),
        P(("dp", "mp"), None),
        P(("dp", "mp"), None),
        P(("dp", "mp"), None),
        P(("dp", "mp"), None),
        P(("dp", "mp"), None),
        P(("dp", "mp"), None),
    )
    return jax.shard_map(
        per_device,
        mesh=mesh,
        in_specs=placed,
        out_specs=(P(("dp", "mp"), None), P(("dp", "mp"), None), P()),
        check_vma=False,
    )
```

profile of v0, /device:TPU:0, one launch (start us, length us, event | category | flops | bytes accessed | tf_op | source)
XLA Modules:
  0.0 275.2 jit_solution(15147655237037164146)
XLA Ops:
  7.2 0.0 all-gather.2.cloned.1.call-start
  7.2 1.8 convert_bitcast_fusion
  9.0 1.2 pad_maximum_fusion.1
  10.2 0.0 copy-start.6
  10.2 0.0 copy-start.5
  10.2 0.0 all-gather.2.cloned.1.call-update
  10.2 0.0 reduce-scatter.2.cloned.1.call-start
  10.3 0.6 copy-done.6
  10.9 0.6 reduce_sum.56
  12.2 0.7 dynamic-slice_reduce_fusion
  12.9 0.6 iota_compare_fusion
  13.6 0.0 copy-start.4
  13.6 95.4 %all-gather.2.cloned.1.call-done = bf16[2,768,1664]{2,1,0:T(8,128)(2,1)} async-done(((bf16[2,192,1664]{2,1,0:T(8,128)(2,1)}), bf16[2,768,1664]{2,1,0:T(8,128)(2,1)}) %all-gather.2.cloned.1.call-update) | async-done | bytes 5111824 | tf_op jit(solution)/shard_map/all_gather | solution.py:64
  109.0 0.0 copy-done.5
  109.0 2.5 fusion
  111.5 0.0 copy-done.4
  111.6 0.9 multiply_convert_fusion
  112.5 5.3 %multiply_convert_fusion.1 = bf16[768,1664]{1,0:T(8,128)(2,1)} fusion(f32[]{:T(128)S(6)} %div.30, bf16[2,768,1664]{2,1,0:T(8,128)(2,1)} %all-gather.2.cloned.1.call-done, f32[48,768]{1,0:T(8,128)S(1)} %fusion, bf16[48,1664]{1,0:T(8,128)(2,1)S(1)} %copy-done.4, pred[48]{0:T(512)(128)(4,1)S(1)} %iota_compare_fusion, bf16[48,1664]{1,0:T(8,128)(2,1)S(1)} %copy-done.5), kind=kOutput, calls=%fused_computation.2 | convolution fusion | flops 248524800 | bytes 5579780 | tf_op jit(solution)/shard_map/dot_general | solution.py:81
  117.8 4.3 %pad_maximum_fusion = bf16[768,3328]{1,0:T(8,128)(2,1)} fusion(bf16[768,1664]{1,0:T(8,128)(2,1)S(1)} %multiply_convert_fusion, bf16[768,1664]{1,0:T(8,128)(2,1)} %multiply_convert_fusion.1), kind=kLoop, calls=%fused_computation | loop fusion | flops 10223616 | bytes 10223616 | tf_op jit(solution)/shard_map/concatenate | solution.py:88
  122.1 0.0 reduce-scatter.2.cloned.1.call-update
  122.1 0.0 copy-start
  122.1 0.0 copy-start.1
  122.2 90.1 %reduce-scatter.2.cloned.1.call-done = bf16[192,3328]{1,0:T(8,128)(2,1)} async-done(((bf16[768,3328]{1,0:T(8,128)(2,1)}), bf16[192,3328]{1,0:T(8,128)(2,1)}) %reduce-scatter.2.cloned.1.call-update) | async-done | bytes 1277968 | tf_op jit(solution)/shard_map/reduce_scatter | solution.py:87
  212.3 0.0 copy-start.3
  212.3 1.6 convert_element_type.24
  213.9 0.0 copy-done
  213.9 0.0 copy-done.1
  213.9 0.1 copy-done.3
  214.0 6.3 %multiply_reduce_fusion = (f32[]{:T(128)}, f32[192,1664]{1,0:T(8,128)}, f32[]{:T(128)}, f32[192,1664]{1,0:T(8,128)}, f32[]{:T(128)}, /*index=5*/f32[]{:T(128)}) fusion(f32[192,1664]{1,0:T(8,128)S(1)} %copy-done.1, f32[192,1664]{1,0:T(8,128)S(1)} %copy-done.3, f32[192,3328]{1,0:T(8,128)S(1)} %convert_element_type.24, f32[192,1664]{1,0:T(8,128)} %param.16, ...), kind=kLoop, calls=%fused_computation.23 | loop fusion | flops 10862588 | bytes 12779536 | tf_op jit(solution)/shard_map/reduce_sum | solution.py:100
  220.3 41.0 %all-reduce = (f32[]{:T(128)}, f32[]{:T(128)}, f32[]{:T(128)}, f32[]{:T(128)}) all-reduce(f32[]{:T(128)} %get-tuple-element.13, f32[]{:T(128)} %get-tuple-element.11, f32[]{:T(128)} %get-tuple-element.14, f32[]{:T(128)} %get-tuple-element.7), channel_id=1, replica_groups=mesh['dp'=4,'mp'=8] {'dp','mp'}, use_global_device_ids=true, to_apply=%region_1.0 | all-reduce | flops 4 | bytes 32 | tf_op jit(solution)/shard_map/psum | solution.py:95
  263.9 0.0 copy-start.2
  263.9 2.6 multiply_subtract_fusion.1
  266.5 0.0 copy-done.2
  266.5 1.3 multiply_subtract_fusion
  267.8 0.6 pad_maximum_fusion.2
Async XLA Ops:
  7.2 101.8 %all-gather.2.cloned.1.call-start = ((), (), s32[]{:S(2)}) async-start(), calls=%async_computation.1 | async-start | bytes 6389760 | tf_op jit(solution)/shard_map/all_gather | solution.py:64
  10.2 0.7 copy-start.6
  10.2 98.8 %copy-start.5 = (bf16[48,1664]{1,0:T(8,128)(2,1)S(1)}, bf16[48,1664]{1,0:T(8,128)(2,1)}, u32[]{:S(2)}) copy-start(bf16[48,1664]{1,0:T(8,128)(2,1)} %param.10) | copy-start | bytes 479236
  10.2 202.1 %reduce-scatter.2.cloned.1.call-start = ((), (), s32[]{:S(2)}) async-start(), calls=%async_computation.2 | async-start | bytes 6389760 | tf_op jit(solution)/shard_map/reduce_scatter | solution.py:87
  13.6 98.0 %copy-start.4 = (bf16[48,1664]{1,0:T(8,128)(2,1)S(1)}, bf16[48,1664]{1,0:T(8,128)(2,1)}, u32[]{:S(2)}) copy-start(bf16[48,1664]{1,0:T(8,128)(2,1)} %param.11) | copy-start | bytes 479236
  122.1 91.8 %copy-start = (f32[192,1664]{1,0:T(8,128)S(1)}, f32[192,1664]{1,0:T(8,128)}, u32[]{:S(2)}) copy-start(f32[192,1664]{1,0:T(8,128)} %param.13) | copy-start | bytes 3833860
  122.1 91.7 %copy-start.1 = (f32[192,1664]{1,0:T(8,128)S(1)}, f32[192,1664]{1,0:T(8,128)}, u32[]{:S(2)}) copy-start(f32[192,1664]{1,0:T(8,128)} %param.14) | copy-start | bytes 3833860
  212.3 1.7 copy-start.3
  263.9 2.6 copy-start.2
Sparse Core Ops, SparseCore 0:
  10.4 98.5 all-gather.1
  122.3 90.0 reduce-scatter.1
where the time goes:
time: 276 us; the launch traced here: 275 us
  waiting for transfers between devices  186 us (67%)
  blocking collectives  41 us (15%)
  other arithmetic  21.6 us (8%)
  between operations  17.5 us (6%)
  matrix products  8.74 us (3%)
    all_gather x1, waiting for transfers between devices, per_device(): piece = lax.all_gather(stacked, 'dp', axis=1, tiled=True)  95.4 us
    reduce_scatter x1, waiting for transfers between devices, per_device(): lax.psum_scatter(jnp.concatenate([up_term, down_term], 1).astype(jnp.bflo...  90.1 us
    psum x1, blocking collectives, per_device(): lax.psum((jnp.sum(up_weight * up_weight), jnp.sum(update_up * update_up),...  41 us
    reduce_sum x1, other arithmetic, per_device(): jnp.sum(update_down * update_down)  6.27 us
  transfers between devices with their start and end apart: 2, of which 2 were waited for; matrix products, arithmetic and copies ran while one was open for 1% of the time, Pallas kernels for 0%

commit v1 on v0

--- a/solution.py
+++ b/solution.py
@@ -16,6 +16,16 @@
 norm_eps = 1e-06
 decay_rate = 0.05
 learn_rate = 0.02
+
+
+def turned_line(x, mesh_axis, dim):
+    devices = lax.axis_size(mesh_axis)
+    held, blocks = (x, [x])
+    for _ in range(devices - 1):
+        held = lax.ppermute(held, mesh_axis, [(i, (i + 1) % devices) for i in range(devices)])
+        blocks.insert(0, held)
+    line = jnp.concatenate(blocks, axis=dim)
+    return jnp.roll(line, (lax.axis_index(mesh_axis) + 1) * x.shape[dim], axis=dim)
 
 
 def gelu_exact(value):
@@ -61,7 +71,7 @@
     inputs = jnp.where(inside, features, jnp.zeros_like(features))
     cotangent = jnp.where(inside, output_grad, jnp.zeros_like(output_grad))
     stacked = jnp.stack([up_weight.astype(jnp.bfloat16), down_weight.astype(jnp.bfloat16)])
-    piece = lax.all_gather(stacked, "dp", axis=1, tiled=True)
+    piece = turned_line(stacked, "dp", 1)
     pre_part = (
         lax.dot_general(
             inputs, piece[0], (((1,), (1,)), ((), ())), preferred_element_type=jnp.float32

time: 276 us -> 279 us (1.011)
  local copies, waits for them, and re-layouts: 0.72 us -> 10.3 us
  waiting for transfers between devices: 186 us -> 179 us
  starting transfers between devices: 0.08 us -> 3.15 us
    all_gather x1 -> x0, waiting for transfers between devices: 95.4 us -> none  [per_device(): piece = lax.all_gather(stacked, 'dp', axis=1, tiled=True)]
    ppermute x0 -> x3, waiting for transfers between devices: none -> 89 us  [turned_line(): lax.ppermute(held, mesh_axis, [(i, (i + 1) % devices) for i in range(devi...]
    unnamed x14 -> x22, local copies, waits for them, and re-layouts: 0.72 us -> 10.3 us
    ppermute x0 -> x3, starting transfers between devices: none -> 3.11 us  [turned_line(): lax.ppermute(held, mesh_axis, [(i, (i + 1) % devices) for i in range(devi...]
  transfers between devices with their start and end apart: 2 -> 4, of which waited for: 2 -> 4; matrix products, arithmetic and copies ran while one was open for 1% -> 1% of each run, Pallas kernels for 0% -> 0%
where the time goes in v1:
time: 279 us; the launch traced here: 278 us
  waiting for transfers between devices  179 us (64%)
  blocking collectives  41 us (15%)
  other arithmetic  20.9 us (7%)
  between operations  17.5 us (6%)
  local copies, waits for them, and re-layouts  10.3 us (4%)
  matrix products  7.05 us (3%)
  starting transfers between devices  3.15 us (1%)
    reduce_scatter x1, waiting for transfers between devices, per_device(): lax.psum_scatter(jnp.concatenate([up_term, down_term], 1).astype(jnp.bflo...  89.6 us
    ppermute x3, waiting for transfers between devices, turned_line(): lax.ppermute(held, mesh_axis, [(i, (i + 1) % devices) for i in range(devi...  89 us
    psum x1, blocking collectives, per_device(): lax.psum((jnp.sum(up_weight * up_weight), jnp.sum(update_up * update_up),...  41 us
    unnamed x22, local copies, waits for them, and re-layouts  10.3 us
    reduce_sum x1, other arithmetic, per_device(): jnp.sum(update_down * update_down)  6.27 us
  transfers between devices with their start and end apart: 4, of which 4 were waited for; matrix products, arithmetic and copies ran while one was open for 1% of the time, Pallas kernels for 0%

profile of v1, /device:TPU:0, one launch (start us, length us, event | category | flops | bytes accessed | tf_op | source)
XLA Modules:
  0.0 278.5 jit_solution(5057369126650512208)
XLA Ops:
  7.2 0.0 reduce-scatter.2.cloned.1.call-start
  7.2 1.8 convert_bitcast_fusion
  9.0 0.0 copy-start.7
  9.0 0.1 pad_maximum_fusion.1
  9.2 3.1 %collective-permute-start = (bf16[2,192,1664]{2,1,0:T(8,128)(2,1)S(1)}, bf16[2,192,1664]{2,1,0:T(8,128)(2,1)S(1)}, u32[]{:S(2)}, u32[]{:S(2)}) collective-permute-start(bf16[2,192,1664]{2,1,0:T(8,128)(2,1)S(1)} %pad_maximum_fusion.1), channel_id=1, source_target_pairs={{0,8},{8,16},{16,24},{24,0},{1,9},{9,17},{17,25},{25,1},{2,10},{10... | collective-permute-start | bytes 3833864 | tf_op jit(solution)/shard_map/ppermute | solution.py:25
  12.3 30.1 %collective-permute-done = bf16[2,192,1664]{2,1,0:T(8,128)(2,1)S(1)} collective-permute-done((bf16[2,192,1664]{2,1,0:T(8,128)(2,1)S(1)}, bf16[2,192,1664]{2,1,0:T(8,128)(2,1)S(1)}, u32[]{:S(2)}, u32[]{:S(2)}) %collective-permute-start) | collective-permute-done | bytes 1277984 | tf_op jit(solution)/shard_map/ppermute | solution.py:25
  42.4 0.0 collective-permute-start.1
  42.4 31.1 %collective-permute-done.1 = bf16[2,192,1664]{2,1,0:T(8,128)(2,1)} collective-permute-done((bf16[2,192,1664]{2,1,0:T(8,128)(2,1)S(1)}, bf16[2,192,1664]{2,1,0:T(8,128)(2,1)}, u32[]{:S(2)}, u32[]{:S(2)}) %collective-permute-start.1) | collective-permute-done | bytes 1277984 | tf_op jit(solution)/shard_map/ppermute | solution.py:25
  73.5 0.0 collective-permute-start.2
  73.5 0.0 copy-done.7
  73.5 0.6 reduce_sum.56
  74.2 0.7 dynamic-slice_reduce_fusion
  75.6 0.7 iota_compare_fusion
  76.3 27.8 %collective-permute-done.2 = bf16[2,192,1664]{2,1,0:T(8,128)(2,1)} collective-permute-done((bf16[2,192,1664]{2,1,0:T(8,128)(2,1)}, bf16[2,192,1664]{2,1,0:T(8,128)(2,1)}, u32[]{:S(2)}, u32[]{:S(2)}) %collective-permute-start.2) | collective-permute-done | bytes 1277984 | tf_op jit(solution)/shard_map/ppermute | solution.py:25
  104.0 1.4 constant_dynamic-update-slice_fusion.7
  105.4 1.5 constant_dynamic-update-slice_fusion.6
  106.9 0.2 constant_dynamic-update-slice_fusion.5
  107.1 0.2 constant_dynamic-update-slice_fusion.4
  107.3 1.5 constant_dynamic-update-slice_fusion.3
  108.8 1.5 constant_dynamic-update-slice_fusion.2
  110.3 0.2 constant_dynamic-update-slice_fusion.1
  110.4 0.0 copy-start.5
  110.5 0.2 constant_dynamic-update-slice_fusion
  110.6 0.0 copy-start.3
  110.7 3.9 %copy-done.3 = bf16[2,1536,1664]{2,1,0:T(8,128)(2,1)} copy-done((bf16[2,1536,1664]{2,1,0:T(8,128)(2,1)}, bf16[2,1536,1664]{2,1,0:T(8,128)(2,1)S(1)}, u32[]{:S(2)}) %copy-start.3) | copy-done | bytes 10223640
  114.5 0.0 copy-done.5
  114.5 0.0 copy-start.6
  114.5 0.8 fusion
  115.4 0.1 copy-done.6
  115.4 0.9 multiply_convert_fusion
  116.3 5.3 %multiply_convert_fusion.1 = bf16[768,1664]{1,0:T(8,128)(2,1)} fusion(f32[]{:T(128)S(6)} %div.30, bf16[2,1536,1664]{2,1,0:T(8,128)(2,1)} %copy-done.3, s32[]{:T(128)S(6)} %add.79, s32[]{:T(128)S(6)} %select_n.26, f32[48,768]{1,0:T(8,128)S(1)} %fusion, bf16[48,1664]{1,0:T(8,128)(2,1)S(1)} %copy-done.6, pred[48]{0:T(512)(128)(4,1)S(1)} %iota_compare_fusion, ...), kind=kOutput, calls=%fused_computation.2 | convolution fusion | flops 248524800 | bytes 5579788 | tf_op jit(solution)/shard_map/dot_general | solution.py:91
  121.7 4.3 %pad_maximum_fusion = bf16[768,3328]{1,0:T(8,128)(2,1)} fusion(bf16[768,1664]{1,0:T(8,128)(2,1)S(1)} %multiply_convert_fusion, bf16[768,1664]{1,0:T(8,128)(2,1)} %multiply_convert_fusion.1), kind=kLoop, calls=%fused_computation | loop fusion | flops 10223616 | bytes 10223616 | tf_op jit(solution)/shard_map/concatenate | solution.py:98
  126.0 0.0 reduce-scatter.2.cloned.1.call-update
  126.0 0.0 copy-start
  126.0 0.0 copy-start.1
  126.0 89.6 %reduce-scatter.2.cloned.1.call-done = bf16[192,3328]{1,0:T(8,128)(2,1)} async-done(((bf16[768,3328]{1,0:T(8,128)(2,1)}), bf16[192,3328]{1,0:T(8,128)(2,1)}) %reduce-scatter.2.cloned.1.call-update) | async-done | bytes 1277968 | tf_op jit(solution)/shard_map/reduce_scatter | solution.py:97
  215.6 0.0 copy-start.4
  215.6 1.6 convert_element_type.24
  217.2 0.0 copy-done
  217.2 0.0 copy-done.1
  217.2 0.1 copy-done.4
  217.3 6.3 %multiply_reduce_fusion = (f32[]{:T(128)}, f32[192,1664]{1,0:T(8,128)}, f32[]{:T(128)}, f32[192,1664]{1,0:T(8,128)}, f32[]{:T(128)}, /*index=5*/f32[]{:T(128)}) fusion(f32[192,1664]{1,0:T(8,128)S(1)} %copy-done, f32[192,1664]{1,0:T(8,128)S(1)} %copy-done.4, f32[192,3328]{1,0:T(8,128)S(1)} %convert_element_type.24, f32[192,1664]{1,0:T(8,128)} %param.16, ...), kind=kLoop, calls=%fused_computation.23 | loop fusion | flops 10862588 | bytes 12779536 | tf_op jit(solution)/shard_map/reduce_sum | solution.py:110
  223.5 41.0 %all-reduce = (f32[]{:T(128)}, f32[]{:T(128)}, f32[]{:T(128)}, f32[]{:T(128)}) all-reduce(f32[]{:T(128)} %get-tuple-element.13, f32[]{:T(128)} %get-tuple-element.11, f32[]{:T(128)} %get-tuple-element.14, f32[]{:T(128)} %get-tuple-element.7), channel_id=1, replica_groups=mesh['dp'=4,'mp'=8] {'dp','mp'}, use_global_device_ids=true, to_apply=%region_1.0 | all-reduce | flops 4 | bytes 32 | tf_op jit(solution)/shard_map/psum | solution.py:105
  267.2 0.6 pad_maximum_fusion.2
  267.8 0.0 copy-start.2
  267.8 2.6 multiply_subtract_fusion
  270.4 0.0 copy-done.2
  270.4 1.3 multiply_subtract_fusion.1
Async XLA Ops:
  7.2 208.4 %reduce-scatter.2.cloned.1.call-start = ((), (), s32[]{:S(2)}) async-start(), calls=%async_computation.1 | async-start | bytes 6389760 | tf_op jit(solution)/shard_map/reduce_scatter | solution.py:97
  9.0 64.5 %copy-start.7 = (s32[16]{0:T(128)S(1)}, s32[16]{0:T(128)}, u32[]{:S(2)}) copy-start(s32[16]{0:T(128)} %param.12) | copy-start | bytes 196
  9.2 33.2 %collective-permute-start = (bf16[2,192,1664]{2,1,0:T(8,128)(2,1)S(1)}, bf16[2,192,1664]{2,1,0:T(8,128)(2,1)S(1)}, u32[]{:S(2)}, u32[]{:S(2)}) collective-permute-start(bf16[2,192,1664]{2,1,0:T(8,128)(2,1)S(1)} %pad_maximum_fusion.1), channel_id=1, source_target_pairs={{0,8},{8,16},{16,24},{24,0},{1,9},{9,17},{17,25},{25,1},{2,10},{10... | collective-permute-start | bytes 3833864 | tf_op jit(solution)/shard_map/ppermute | solution.py:25
  42.4 31.1 %collective-permute-start.1 = (bf16[2,192,1664]{2,1,0:T(8,128)(2,1)S(1)}, bf16[2,192,1664]{2,1,0:T(8,128)(2,1)}, u32[]{:S(2)}, u32[]{:S(2)}) collective-permute-start(bf16[2,192,1664]{2,1,0:T(8,128)(2,1)S(1)} %collective-permute-done), channel_id=1, source_target_pairs={{0,8},{8,16},{16,24},{24,0},{1,9},{9,17},{17,25},{25,1},{2,10},{10... | collective-permute-start | bytes 3833864 | tf_op jit(solution)/shard_map/ppermute | solution.py:25
  73.5 30.5 %collective-permute-start.2 = (bf16[2,192,1664]{2,1,0:T(8,128)(2,1)}, bf16[2,192,1664]{2,1,0:T(8,128)(2,1)}, u32[]{:S(2)}, u32[]{:S(2)}) collective-permute-start(bf16[2,192,1664]{2,1,0:T(8,128)(2,1)} %collective-permute-done.1), channel_id=1, source_target_pairs={{0,8},{8,16},{16,24},{24,0},{1,9},{9,17},{17,25},{25,1},{2,10},{10... | collective-permute-start | bytes 3833864 | tf_op jit(solution)/shard_map/ppermute | solution.py:25
  110.4 4.1 %copy-start.5 = (bf16[48,1664]{1,0:T(8,128)(2,1)S(1)}, bf16[48,1664]{1,0:T(8,128)(2,1)}, u32[]{:S(2)}) copy-start(bf16[48,1664]{1,0:T(8,128)(2,1)} %param.10) | copy-start | bytes 479236
  110.6 3.9 %copy-start.3 = (bf16[2,1536,1664]{2,1,0:T(8,128)(2,1)}, bf16[2,1536,1664]{2,1,0:T(8,128)(2,1)S(1)}, u32[]{:S(2)}) copy-start(bf16[2,1536,1664]{2,1,0:T(8,128)(2,1)S(1)} %constant_dynamic-update-slice_fusion) | copy-start | bytes 30670852
  114.5 0.9 copy-start.6
  126.0 91.2 %copy-start = (f32[192,1664]{1,0:T(8,128)S(1)}, f32[192,1664]{1,0:T(8,128)}, u32[]{:S(2)}) copy-start(f32[192,1664]{1,0:T(8,128)} %param.14) | copy-start | bytes 3833860
  126.0 91.2 %copy-start.1 = (f32[192,1664]{1,0:T(8,128)S(1)}, f32[192,1664]{1,0:T(8,128)}, u32[]{:S(2)}) copy-start(f32[192,1664]{1,0:T(8,128)} %param.13) | copy-start | bytes 3833860
  215.6 1.7 copy-start.4
  267.8 2.6 copy-start.2
Sparse Core Ops, SparseCore 0:
  126.1 89.4 reduce-scatter.1
